TPU v7x, 256 devices: a whole 4x4x8 slice. The times are simulated.
256 devices in a mesh: leaf: 2 (over core), row: 16 (over z, x_lo), col: 8 (over y, x_hi).
Axes of the slice: x: 4 (x_hi: 2, x_lo: 2; x = x_hi * 2 + x_lo), y: 4, z: 8, core: 2. Of those that a mesh axis runs over, the one named last changes fastest.
Arguments:
- child_tiles: float32 [1024, 64, 4096], P(('leaf', 'row'), None, 'col'), may hold values from -0.078125 to 0.078125
- block_mask: int32 [1024, 64], P(('leaf', 'row'), 'col'), may hold values 0 or 1
- destination: int32 [1024, 1], P(('leaf', 'row')), may hold values from 0 to 31; in each aligned block of 32 rows (0 to 31, 32 to 63, ...) at most 2 rows name the same one
Outputs:
- r_top: float32 [2, 128, 4096], P('leaf', None, 'col')
Inputs may be any that keep to these rules, and one draw needn't show every extreme that they name: Among the tiles of one device, no destination is named more than 2 times, a bound that some block reaches.
All inputs are finite; a program needn't handle non-finite values. No bound on the sum of `block_mask` on one device may be relied on, other than what follows from the above.
Results may differ from a plain program's by a relative error of at most 0.0003.
Values sent between devices are 32-bit elements; how exact they have to be, the bound alone decides.
A program may use at most 64 MiB of HBM per device.

v0:
```python
import jax
import jax.numpy as jnp
from jax import lax
from jax.sharding import PartitionSpec as P

FRONTS = 2


def per_device(child_tiles, block_mask, destination):
    tile_count, edge, columns_dev = child_tiles.shape
    blocks_dev = columns_dev // edge
    col = lax.axis_index("col")
    per_front = lax.axis_size("row")
    mask = block_mask.astype(jnp.float32)
    rows = tile_count * edge
    tiles = child_tiles.reshape(rows, columns_dev)
    own = tiles[:, :edge] * jnp.repeat(mask[:, 0], edge)[:, None]
    panel = jnp.concatenate([jnp.where(col == k, own, 0.0) for k in range(2)], axis=1)
    panel = lax.psum(panel, "col")
    front = jnp.repeat(destination[:, 0] // per_front, edge)[:, None]
    left = jnp.concatenate([jnp.where(front == f, panel, 0.0) for f in range(FRONTS)], axis=1)
    masked = (tiles.reshape(tile_count, edge, blocks_dev, edge) * mask[:, None, :, None]).reshape(
        rows, columns_dev
    )
    dot = lambda a, b: lax.dot_general(
        a, b, (((0,), (0,)), ((), ())), precision=lax.Precision.HIGHEST
    )
    sums = jnp.concatenate([dot(left, masked), dot(left, panel)], axis=1)
    sums = lax.psum_scatter(sums, "leaf", scatter_dimension=0, tiled=True)
    sums = lax.psum(sums, "row")
    cross, gram = (sums[:, :columns_dev], sums[:, columns_dev:])
    lower = jnp.linalg.cholesky(gram)
    top = lax.linalg.triangular_solve(lower, cross, left_side=True, lower=True)
    col_count = lax.axis_size("col")
    place = jnp.repeat(jnp.arange(blocks_dev) * col_count + col, edge)
    line = jnp.arange(2 * edge) // edge
    return jnp.where(place[None, :] >= line[:, None], top, 0.0)[None]


def solution(mesh):
    in_specs = (
        P(("leaf", "row"), None, "col"),
        P(("leaf", "row"), "col"),
        P(("leaf", "row"), None),
    )
    return jax.shard_map(
        per_device, mesh=mesh, in_specs=in_specs, out_specs=P("leaf", None, "col"), check_vma=False
    )
```

profile of v0, /device:TPU:6, one launch (start us, length us, event | category | flops | bytes accessed | tf_op | source)
XLA Modules:
  0.0 309.4 jit_solution(1366986369914015669)
XLA Ops:
  6.5 0.7 convert_element_type.3
  7.2 0.1 broadcast_in_dim.48
  7.3 0.1 mul.25
  7.4 1.6 fusion.5
  9.0 1.3 pad_maximum_fusion.3
  10.3 0.0 all-reduce.3.cloned.1.call-update
  10.3 0.0 reduce-scatter.2.cloned.1.call-start
  10.3 0.1 copy.4
  10.5 0.1 broadcast_in_dim.51
  10.5 0.1 eq.37
  10.6 0.1 broadcast_in_dim.46
  10.7 0.1 eq.33
  10.8 3.8 %mul.28 = f32[32,64,8,64]{3,2,1,0:T(8,128)} broadcast(f32[32,8]{1,0:T(8,128)S(1)} %copy.4), dimensions={0,2} | broadcast | bytes 4195328 | tf_op jit(solution)/shard_map/mul | solution.py:22
  14.6 7.5 %mul.29 = f32[2048,512]{1,0:T(8,128)} reshape(f32[32,64,8,64]{3,2,1,0:T(8,128)} %mul.28) | data formatting | bytes 8388608 | tf_op jit(solution)/shard_map/mul | solution.py:22
  22.1 84.0 %all-reduce.3.cloned.1.call-done = f32[2048,128]{1,0:T(8,128)} async-done(((f32[2048,128]{1,0:T(8,128)}), f32[2048,128]{1,0:T(8,128)}) %all-reduce.3.cloned.1.call-update) | async-done | bytes 1048592 | tf_op jit(solution)/shard_map/psum | solution.py:19
  106.1 2.8 broadcast_select_fusion.1
  109.0 9.4 %fusion = f32[256,512]{0,1:T(8,128)S(1)} fusion(f32[2048,512]{1,0:T(8,128)} %bitcast.27, f32[2048,512]{1,0:T(8,128)} %mul.29, f32[2048,128]{1,0:T(8,128)S(1)} %get-tuple-element.10, f32[2048,128]{1,0:T(8,128)S(1)} %get-tuple-element.9), kind=kOutput, calls=%fused_computation | convolution fusion | flops 3222798336 | bytes 11010048 | tf_op jit(solution)/shard_map/dot_general | solution.py:25
  118.4 1.9 fusion.2
  120.3 0.9 pad_maximum_fusion.4
  121.2 0.2 all-reduce.5.cloned.1.call-start
  121.4 14.5 %reduce-scatter.2.cloned.1.call-done = f32[128,640]{0,1:T(8,128)} async-done(((f32[256,640]{0,1:T(8,128)}), f32[128,640]{0,1:T(8,128)}) %reduce-scatter.2.cloned.1.call-update) | async-done | bytes 327696 | tf_op jit(solution)/shard_map/reduce_scatter | solution.py:29
  136.0 0.1 broadcast_in_dim.45
  136.1 0.1 ge.17
  136.2 140.0 %all-reduce.5.cloned.1.call-done = f32[128,640]{0,1:T(8,128)} async-done(((f32[128,640]{0,1:T(8,128)}), f32[128,640]{0,1:T(8,128)}) %all-reduce.5.cloned.1.call-update) | async-done | bytes 327696 | tf_op jit(solution)/shard_map/psum | solution.py:30
  276.1 0.8 slice.25
  277.0 0.1 copy.6
  277.1 0.9 fusion.9
  277.9 11.7 %cholesky.16 = f32[128,128]{1,0:T(8,128)S(1)} custom-call(f32[128,128]{1,0:T(8,128)S(1)} %fusion.9), custom_call_target="Cholesky" | custom-call | tf_op jit(solution)/shard_map/jit(cholesky)/cholesky | solution.py:32
  289.7 0.6 compare_reduce_fusion
  290.3 0.7 fusion.7
  291.0 9.8 %custom-call.6 = f32[1,128,128]{1,2,0:T(8,128)S(1)} custom-call(f32[1,128,128]{2,1,0:T(8,128)S(1)} %fusion.7), custom_call_target="InvertDiagBlocksLowerTriangular" | custom-call | tf_op jit(solution)/shard_map/triangular_solve | solution.py:33
  300.8 2.1 fusion.3
  (13 shorter events, 0.1 us)
Async XLA Ops:
  6.5 3.9 %copy-start.1 = (s32[32,1]{0,1:T(1,128)S(1)}, s32[32,1]{0,1:T(1,128)}, u32[]{:S(2)}) copy-start(s32[32,1]{0,1:T(1,128)} %param.5) | copy-start | bytes 388
  6.5 99.6 %all-reduce.3.cloned.1.call-start = ((), (), s32[]{:S(2)}) async-start(), calls=%async_computation.1 | async-start | bytes 2097152 | tf_op jit(solution)/shard_map/psum | solution.py:19
  10.3 125.7 %reduce-scatter.2.cloned.1.call-start = ((), (), s32[]{:S(2)}) async-start(), calls=%async_computation.2 | async-start | bytes 983040 | tf_op jit(solution)/shard_map/reduce_scatter | solution.py:29
  109.0 9.4 %copy-start = (f32[2048,128]{1,0:T(8,128)S(1)}, f32[2048,128]{1,0:T(8,128)}, u32[]{:S(2)}) copy-start(f32[2048,128]{1,0:T(8,128)} %all-reduce.3.cloned.1.call-done) | copy-start | bytes 3145732
  121.2 154.9 %all-reduce.5.cloned.1.call-start = ((), (), s32[]{:S(2)}) async-start(), calls=%async_computation.3 | async-start | bytes 655360 | tf_op jit(solution)/shard_map/psum | solution.py:30
Sparse Core Ops, SparseCore 0:
  10.4 95.6 all-reduce.2
  121.3 14.6 reduce-scatter.1
  138.6 137.4 all-reduce.4
where the time goes:
time: 310 us; the launch traced here: 309 us
  waiting for transfers between devices  239 us (77%)
  other arithmetic  31 us (10%)
  matrix products  13.4 us (4%)
  between operations  13.2 us (4%)
  local copies, waits for them, and re-layouts  13 us (4%)
    psum x1, waiting for transfers between devices, per_device(): sums = lax.psum(sums, 'row')  140 us
    psum x1, waiting for transfers between devices, per_device(): panel = lax.psum(panel, 'col')  84 us
    reduce_scatter x1, waiting for transfers between devices, per_device(): sums = lax.psum_scatter(sums, 'leaf', scatter_dimension=0, tiled=True)  14.5 us
    another operation x3, other arithmetic, per_device(): lower = jnp.linalg.cholesky(gram)  12.4 us
    mul x2, local copies, waits for them, and re-layouts, per_device(): tiles.reshape(tile_count, edge, blocks_dev, edge) * mask[:, None, :, None]  11.3 us
    dot_general x2, matrix products, per_device(): lax.dot_general(a, b, (((0,), (0,)), ((), ())), precision=lax.Precision.H...  11.3 us
    another operation x2, other arithmetic, per_device(): top = lax.linalg.triangular_solve(lower, cross, left_side=True, lower=True)  10.5 us
  transfers between devices with their start and end apart: 3, of which 3 were waited for; matrix products, arithmetic and copies ran while one was open for 4% of the time, Pallas kernels for 0%

commit v1 on v0

--- a/solution.py
+++ b/solution.py
@@ -27,7 +27,7 @@
     )
     sums = jnp.concatenate([dot(left, masked), dot(left, panel)], axis=1)
     sums = lax.psum_scatter(sums, "leaf", scatter_dimension=0, tiled=True)
-    sums = lax.psum(sums, "row")
+    sums = lax.all_gather(sums, "row").sum(axis=0)
     cross, gram = (sums[:, :columns_dev], sums[:, columns_dev:])
     lower = jnp.linalg.cholesky(gram)
     top = lax.linalg.triangular_solve(lower, cross, left_side=True, lower=True)

time: 310 us -> 296 us (0.955)
  waiting for transfers between devices: 239 us -> 221 us
    psum x1 -> x0, waiting for transfers between devices: 140 us -> none  [per_device(): sums = lax.psum(sums, 'row')]
    all_gather x0 -> x1, waiting for transfers between devices: none -> 122 us  [per_device(): sums = lax.all_gather(sums, 'row').sum(axis=0)]
where the time goes in v1:
time: 296 us; the launch traced here: 293 us
  waiting for transfers between devices  221 us (75%)
  other arithmetic  32.9 us (11%)
  matrix products  13.9 us (5%)
  between operations  13.2 us (4%)
  local copies, waits for them, and re-layouts  12.1 us (4%)
    all_gather x1, waiting for transfers between devices, per_device(): sums = lax.all_gather(sums, 'row').sum(axis=0)  122 us
    psum x1, waiting for transfers between devices, per_device(): panel = lax.psum(panel, 'col')  84 us
    reduce_scatter x1, waiting for transfers between devices, per_device(): sums = lax.psum_scatter(sums, 'leaf', scatter_dimension=0, tiled=True)  14.5 us
    dot_general x2, matrix products, per_device(): lax.dot_general(a, b, (((0,), (0,)), ((), ())), precision=lax.Precision.H...  12.8 us
    another operation x3, other arithmetic, per_device(): lower = jnp.linalg.cholesky(gram)  12.4 us
    mul x2, local copies, waits for them, and re-layouts, per_device(): tiles.reshape(tile_count, edge, blocks_dev, edge) * mask[:, None, :, None]  11.3 us
    another operation x2, other arithmetic, per_device(): top = lax.linalg.triangular_solve(lower, cross, left_side=True, lower=True)  10.5 us
  transfers between devices with their start and end apart: 3, of which 3 were waited for; matrix products, arithmetic and copies ran while one was open for 4% of the time, Pallas kernels for 0%

profile of v1, /device:TPU:6, one launch (start us, length us, event | category | flops | bytes accessed | tf_op | source)
XLA Modules:
  0.0 293.4 jit_solution(4315545489613592043)
XLA Ops:
  6.5 0.7 convert_element_type.3
  7.2 0.1 broadcast_in_dim.48
  7.3 0.1 mul.25
  7.4 1.6 fusion.5
  9.0 1.3 pad_maximum_fusion.3
  10.3 0.0 all-reduce.2.cloned.1.call-update
  10.3 0.0 reduce-scatter.2.cloned.1.call-start
  10.3 0.1 copy.7
  10.5 0.1 broadcast_in_dim.51
  10.5 0.1 eq.37
  10.6 0.1 broadcast_in_dim.46
  10.7 0.1 eq.33
  10.8 3.8 %mul.28 = f32[32,64,8,64]{3,2,1,0:T(8,128)} broadcast(f32[32,8]{1,0:T(8,128)S(1)} %copy.7), dimensions={0,2} | broadcast | bytes 4195328 | tf_op jit(solution)/shard_map/mul | solution.py:22
  14.6 7.5 %mul.29 = f32[2048,512]{1,0:T(8,128)} reshape(f32[32,64,8,64]{3,2,1,0:T(8,128)} %mul.28) | data formatting | bytes 8388608 | tf_op jit(solution)/shard_map/mul | solution.py:22
  22.1 84.0 %all-reduce.2.cloned.1.call-done = f32[2048,128]{1,0:T(8,128)} async-done(((f32[2048,128]{1,0:T(8,128)}), f32[2048,128]{1,0:T(8,128)}) %all-reduce.2.cloned.1.call-update) | async-done | bytes 1048592 | tf_op jit(solution)/shard_map/psum | solution.py:19
  106.1 2.8 broadcast_select_fusion.1
  109.0 9.4 %fusion = f32[256,512]{1,0:T(8,128)S(1)} fusion(f32[2048,512]{1,0:T(8,128)} %bitcast.28, f32[2048,512]{1,0:T(8,128)} %mul.29, f32[2048,128]{1,0:T(8,128)S(1)} %get-tuple-element.10, f32[2048,128]{1,0:T(8,128)S(1)} %get-tuple-element.9), kind=kOutput, calls=%fused_computation | convolution fusion | flops 3222798336 | bytes 11010048 | tf_op jit(solution)/shard_map/dot_general | solution.py:25
  118.4 3.4 %fusion.2 = f32[256,128]{1,0:T(8,128)S(1)} fusion(f32[2048,128]{1,0:T(8,128)S(1)} %copy-done, f32[2048,128]{1,0:T(8,128)S(1)} %get-tuple-element.10, f32[2048,128]{1,0:T(8,128)S(1)} %get-tuple-element.9), kind=kOutput, calls=%fused_computation.3 | convolution fusion | flops 805830656 | bytes 3276800 | tf_op jit(solution)/shard_map/dot_general | solution.py:25
  121.8 0.9 pad_maximum_fusion.4
  122.7 0.0 reduce-scatter.2.cloned.1.call-update
  122.7 0.2 all-gather.3.cloned.1.call-start
  122.9 14.5 %reduce-scatter.2.cloned.1.call-done = f32[128,640]{1,0:T(8,128)} async-done(((f32[256,640]{1,0:T(8,128)}), f32[128,640]{1,0:T(8,128)}) %reduce-scatter.2.cloned.1.call-update) | async-done | bytes 327696 | tf_op jit(solution)/shard_map/reduce_scatter | solution.py:29
  137.5 0.1 broadcast_in_dim.45
  137.6 0.1 ge.17
  137.7 122.3 %all-gather.3.cloned.1.call-done = f32[2048,640]{1,0:T(8,128)} async-done(((f32[128,640]{1,0:T(8,128)}), f32[2048,640]{1,0:T(8,128)}) %all-gather.3.cloned.1.call-update) | async-done | bytes 5242896 | tf_op jit(solution)/shard_map/all_gather | solution.py:30
  260.0 2.8 reduce_sum.9
  262.8 0.1 copy.12
  262.9 11.7 %cholesky.16 = f32[128,128]{1,0:T(8,128)S(1)} custom-call(f32[128,128]{1,0:T(8,128)S(1)} %fusion.9), custom_call_target="Cholesky" | custom-call | tf_op jit(solution)/shard_map/jit(cholesky)/cholesky | solution.py:32
  274.7 0.6 compare_reduce_fusion
  275.3 0.7 fusion.7
  276.0 9.8 %custom-call.6 = f32[1,128,128]{1,2,0:T(8,128)S(1)} custom-call(f32[1,128,128]{2,1,0:T(8,128)S(1)} %fusion.7), custom_call_target="InvertDiagBlocksLowerTriangular" | custom-call | tf_op jit(solution)/shard_map/triangular_solve | solution.py:33
  285.8 1.1 fusion.3
  (14 shorter events, 0.1 us)
Async XLA Ops:
  6.5 3.9 %copy-start.1 = (s32[32,1]{0,1:T(1,128)S(1)}, s32[32,1]{0,1:T(1,128)}, u32[]{:S(2)}) copy-start(s32[32,1]{0,1:T(1,128)} %param.5) | copy-start | bytes 388
  6.5 99.6 %all-reduce.2.cloned.1.call-start = ((), (), s32[]{:S(2)}) async-start(), calls=%async_computation.1 | async-start | bytes 2097152 | tf_op jit(solution)/shard_map/psum | solution.py:19
  10.3 127.2 %reduce-scatter.2.cloned.1.call-start = ((), (), s32[]{:S(2)}) async-start(), calls=%async_computation.2 | async-start | bytes 983040 | tf_op jit(solution)/shard_map/reduce_scatter | solution.py:29
  109.0 9.4 %copy-start = (f32[2048,128]{1,0:T(8,128)S(1)}, f32[2048,128]{1,0:T(8,128)}, u32[]{:S(2)}) copy-start(f32[2048,128]{1,0:T(8,128)} %all-reduce.2.cloned.1.call-done) | copy-start | bytes 3145732
  122.7 137.3 %all-gather.3.cloned.1.call-start = ((), (), s32[]{:S(2)}) async-start(), calls=%async_computation.3 | async-start | bytes 5570560 | tf_op jit(solution)/shard_map/all_gather | solution.py:30
Sparse Core Ops, SparseCore 0:
  10.4 95.6 all-reduce.1
  122.8 14.6 reduce-scatter.1
  139.3 120.6 all-gather.2
